TPU v7x, 32 devices: a whole 2x2x4 slice. The times are simulated.
32 devices in a mesh: dp: 4 (over y, x), ctx: 8 (over z, core).
Axes of the slice: x: 2, y: 2, z: 4, core: 2. Of those that a mesh axis runs over, the one named last changes fastest.
Arguments:
- inputs: bfloat16 [4096, 8192], P(('dp', 'ctx')), may hold values from -6 to 6
- out_grad: bfloat16 [4096, 8192], P(('dp', 'ctx')), may hold values from -6 to 6
- b_matrix: bfloat16 [4096, 512], P(('dp', 'ctx')), may hold values from -6 to 6
- c_matrix: bfloat16 [4096, 512], P(('dp', 'ctx')), may hold values from -0.5 to 0.5
- step_raw: bfloat16 [4096, 128], P(('dp', 'ctx'))
- hidden: bfloat16 [4096, 8192], P(('dp', 'ctx')), may hold values from -6 to 6
- log_rates: float32 [128], replicated, may hold values from 0 to 0.6931
- step_bias: float32 [128], replicated
- skip_head_gain: float32 [128], replicated, may hold values from 0.1 to 0.6
- doc_lengths: int32 [4, 4], P('dp'), may hold values from 1 to 512, 1024 in all within a row
- counts: int32 [4], P('dp'), may hold values from 128 to 1024
Outputs:
- grad_inputs: bfloat16 [4096, 8192], P(('dp', 'ctx'))
- grad_b: bfloat16 [4096, 512], P(('dp', 'ctx'))
- grad_c: bfloat16 [4096, 512], P(('dp', 'ctx'))
- grad_steps: bfloat16 [4096, 128], P(('dp', 'ctx'))
- grad_weight: float32 [8192, 128], P(('dp', 'ctx'))
Inputs may be any that keep to these rules, and one draw needn't show every extreme that they name: `doc_lengths`: each sequence's 4 lengths sum to 1024; the longest is exactly 512.
All inputs are finite; a program needn't handle non-finite values.
Results may differ from a plain program's by a relative error of at most 0.0025.
Values may be sent and summed in bfloat16 or wider, within the bound.
No kernel may reach another device: no remote copies, remote signals or barrier semaphores. Data moves between devices by JAX's collectives and lax.ppermute only.
A program may use at most 128 MiB of HBM per device.

v0:
```python
import math

import jax
import jax.numpy as jnp
from jax import lax
from jax.sharding import PartitionSpec as P

P_SIZE = 64
N = 128
BLOCK = 128


HIGHEST = lax.Precision.HIGHEST


def split_blocks(tensor, block_width):
    return tensor.reshape((tensor.shape[0] // block_width, block_width) + tensor.shape[1:])


def decay_tables(log_decay, resets):
    length_q = log_decay.shape[0]
    summed = jnp.moveaxis(jnp.cumsum(log_decay, axis=0), 0, -1)
    segment = jnp.cumsum(resets)
    index_row = jnp.arange(length_q)
    allowed = (index_row[:, None] >= index_row[None, :]) & (segment[:, None] == segment[None, :])
    gap_log = summed[..., :, None] - summed[..., None, :]
    within = jnp.where(allowed, jnp.exp(jnp.minimum(gap_log, 0.0)), 0.0)
    before = jnp.where(segment == 0, jnp.exp(summed), 0.0)
    behind = jnp.where(segment == segment[-1], jnp.exp(summed[..., -1:] - summed), 0.0)
    return (within, before, behind)


def block_ends(values, cotangent, b_rows, c_rows, step_lanes, before, behind):
    b_wide = b_rows.astype(values.dtype)
    c_wide = c_rows.astype(values.dtype)
    state_ends = jnp.einsum(
        "gkq,qgkp,qgn->gkpn", behind * step_lanes, values, b_wide, precision=HIGHEST
    )
    starts = jnp.einsum("gkq,qgkp,qgn->gkpn", before, cotangent, c_wide, precision=HIGHEST)
    return (state_ends, starts)


def block_grads(
    values,
    cotangent,
    b_rows,
    c_rows,
    step_lanes,
    sigmoid_t,
    tables,
    state_in,
    flow_in,
    skip_local,
    neg_rate,
):
    within, before, behind = tables
    b_wide = b_rows.astype(values.dtype)
    c_wide = c_rows.astype(values.dtype)
    length_q = values.shape[0]
    index_row = jnp.arange(length_q)
    upper_mask = (index_row[:, None] >= index_row[None, :]).astype(values.dtype)
    steps_q = jnp.moveaxis(step_lanes, -1, 0)
    before_q = jnp.moveaxis(before, -1, 0)
    behind_q = jnp.moveaxis(behind, -1, 0)
    cross_bc = jnp.einsum("tgn,sgn->gts", c_rows, b_rows, preferred_element_type=jnp.float32)
    pair_dots = jnp.einsum("ugkp,sgkp->gkus", cotangent, values, precision=HIGHEST)
    weighted = within * step_lanes[..., None, :] * pair_dots
    coupled = within * cross_bc[:, None]
    flow_b = jnp.einsum("gkpn,sgn->sgkp", flow_in, b_wide, precision=HIGHEST)
    slope_term = (
        jnp.einsum("gkus,ugkp->sgkp", coupled, cotangent, precision=HIGHEST)
        + behind_q[..., None] * flow_b
    )
    grad_values = steps_q[..., None] * slope_term + skip_local[..., None] * cotangent
    values_flow = jnp.einsum("sgkp,gkpn->sgkn", values, flow_in, precision=HIGHEST)
    grad_b = jnp.einsum("gkus,ugn->sgn", weighted, c_wide, precision=HIGHEST) + jnp.einsum(
        "sgk,sgkn->sgn", steps_q * behind_q, values_flow, precision=HIGHEST
    )
    grad_c = jnp.einsum("gkts,sgn->tgn", weighted, b_wide, precision=HIGHEST) + jnp.einsum(
        "tgk,tgkp,gkpn->tgn", before_q, cotangent, state_in, precision=HIGHEST
    )
    state_c = jnp.einsum("gkpn,ugn->ugkp", state_in, c_wide, precision=HIGHEST)
    direct = jnp.sum(values * slope_term, axis=-1)
    entering = before_q * jnp.sum(cotangent * state_c, axis=-1)
    leaving = behind_q * steps_q * jnp.sum(values * flow_b, axis=-1)
    products = weighted * cross_bc[:, None]
    crossing = jnp.cumsum(products, axis=-1) - products
    crossing_sum = jnp.moveaxis(jnp.sum(crossing * upper_mask, axis=-2), -1, 0)
    entering_sum = jnp.flip(jnp.cumsum(jnp.flip(entering, 0), axis=0), 0)
    leaving_sum = jnp.cumsum(leaving, axis=0) - leaving
    through = before[..., -1] * jnp.sum(flow_in * state_in, axis=(-2, -1))
    decay_grad = crossing_sum + entering_sum + leaving_sum + through
    grad_steps = (direct + neg_rate * decay_grad) * sigmoid_t
    return (grad_values, grad_b, grad_c, grad_steps)


def carry_forward(decays, state_ends, initial):

    def advance(carried, element):
        return (element[0][..., None, None] * carried + element[1], carried)

    last_carry, entering = lax.scan(advance, initial, (decays, state_ends))
    return (entering, last_carry)


def carry_backward(decays, starts, incoming):

    def retreat(carried, element):
        return (element[0][..., None, None] * carried + element[1], carried)

    first_carry, leaving = lax.scan(retreat, incoming, (decays, starts), reverse=True)
    return (leaving, first_carry)


def prepare_blocks(
    values, cotangent, b_rows, c_rows, step_sizes, sigmoid_t, resets, neg_rate, block_width
):
    pieces = tuple(
        (
            split_blocks(tensor, block_width)
            for tensor in (values, cotangent, b_rows, c_rows, step_sizes, sigmoid_t, resets)
        )
    )
    tables = jax.vmap(decay_tables)(pieces[4] * neg_rate, pieces[6])
    step_lanes = jnp.moveaxis(pieces[4], 1, -1)
    state_ends, starts = jax.vmap(block_ends)(
        pieces[0], pieces[1], pieces[2], pieces[3], step_lanes, tables[1], tables[2]
    )
    return (pieces, step_lanes, tables, state_ends, starts)


def finish_blocks(prepared, skip_local, neg_rate, state_in, flow_in):
    pieces, step_lanes, tables, state_ends, starts = prepared
    decays = tables[1][..., -1]
    entering = carry_forward(decays, state_ends, state_in)[0]
    leaving = carry_backward(decays, starts, flow_in)[0]

    def one_block(element):
        return block_grads(
            element[0],
            element[1],
            element[2],
            element[3],
            element[4],
            element[5],
            element[6],
            element[7],
            element[8],
            skip_local,
            neg_rate,
        )

    results = lax.map(
        one_block,
        (
            pieces[0],
            pieces[1],
            pieces[2],
            pieces[3],
            step_lanes,
            pieces[5],
            tables,
            entering,
            leaving,
        ),
    )
    return tuple((tensor.reshape((-1,) + tensor.shape[2:]) for tensor in results))


def local(
    inputs,
    out_grad,
    b_matrix,
    c_matrix,
    step_raw,
    hidden,
    log_rates,
    step_bias,
    skip_head_gain,
    doc_lengths,
    counts,
):
    ctx_size = lax.axis_size("ctx")
    dp_size = lax.axis_size("dp")
    tok_rows = inputs.shape[0]
    head_count = step_raw.shape[1]
    groups = b_matrix.shape[1] // N
    per_group = head_count // groups
    length = tok_rows * ctx_size
    ctx_index = lax.axis_index("ctx")
    count_f = counts.astype(jnp.float32)
    count_total = lax.psum(jnp.sum(count_f), "dp")
    weight = count_f[0] * dp_size / count_total
    lengths_doc = doc_lengths[0]
    starts_doc = jnp.cumsum(lengths_doc) - lengths_doc
    local_heads = head_count // ctx_size
    arrived = (
        lax.all_to_all(inputs, "ctx", split_axis=1, concat_axis=0, tiled=True),
        lax.all_to_all(out_grad, "ctx", split_axis=1, concat_axis=0, tiled=True),
        lax.all_to_all(step_raw, "ctx", split_axis=1, concat_axis=0, tiled=True),
    )
    first_head = ctx_index * local_heads
    group_index = first_head // per_group
    b_all, c_all = (
        lax.all_gather(b_matrix, "ctx", axis=0, tiled=True),
        lax.all_gather(c_matrix, "ctx", axis=0, tiled=True),
    )
    b_rows = lax.dynamic_slice_in_dim(b_all, group_index * N, N, 1).reshape(length, 1, N)
    c_rows = lax.dynamic_slice_in_dim(c_all, group_index * N, N, 1).reshape(length, 1, N)
    values = arrived[0].astype(jnp.float32).reshape(length, 1, local_heads, P_SIZE)
    cotangent = arrived[1].astype(jnp.float32).reshape(length, 1, local_heads, P_SIZE) * weight
    shifted = arrived[2].astype(jnp.float32) + lax.dynamic_slice_in_dim(
        step_bias, first_head, local_heads
    )
    neg_rate = (-jnp.exp(lax.dynamic_slice_in_dim(log_rates, first_head, local_heads))).reshape(
        1, local_heads
    )
    skip_local = lax.dynamic_slice_in_dim(skip_head_gain, first_head, local_heads).reshape(
        1, local_heads
    )
    step_sizes = jax.nn.softplus(shifted).reshape(length, 1, local_heads)
    sigmoid_t = jax.nn.sigmoid(shifted).reshape(length, 1, local_heads)
    positions = jnp.arange(length)
    resets = jnp.any(positions[:, None] == starts_doc[None, :], axis=1).astype(jnp.float32)
    prepared = prepare_blocks(
        values, cotangent, b_rows, c_rows, step_sizes, sigmoid_t, resets, neg_rate, BLOCK
    )
    empty_state = jnp.zeros((1, local_heads, P_SIZE, N), jnp.float32)
    grad_values, grad_b, grad_c, grad_steps = finish_blocks(
        prepared, skip_local, neg_rate, empty_state, empty_state
    )
    grad_inputs, grad_raw = (
        lax.all_to_all(
            grad_values.reshape(length, local_heads * P_SIZE).astype(jnp.bfloat16),
            "ctx",
            split_axis=0,
            concat_axis=1,
            tiled=True,
        ),
        lax.all_to_all(
            grad_steps.reshape(length, local_heads).astype(jnp.bfloat16),
            "ctx",
            split_axis=0,
            concat_axis=1,
            tiled=True,
        ),
    )
    spread = (jnp.arange(groups) == group_index).astype(jnp.float32)
    full_b = (grad_b[:, 0, None, :] * spread[None, :, None]).reshape(length, groups * N)
    full_c = (grad_c[:, 0, None, :] * spread[None, :, None]).reshape(length, groups * N)
    summed_b, summed_c = (
        lax.psum_scatter(full_b, "ctx", scatter_dimension=0, tiled=True),
        lax.psum_scatter(full_c, "ctx", scatter_dimension=0, tiled=True),
    )
    grad_b_out = summed_b.astype(jnp.bfloat16)
    grad_c_out = summed_c.astype(jnp.bfloat16)
    scaling = 1.0 / math.sqrt(dp_size * ctx_size * tok_rows)
    grad_weight = (
        lax.psum_scatter(
            jnp.einsum("td,th->dh", hidden, grad_raw, preferred_element_type=jnp.float32),
            ("dp", "ctx"),
            scatter_dimension=0,
            tiled=True,
        )
        * scaling
    )
    return (grad_inputs, grad_b_out, grad_c_out, grad_raw, grad_weight)


def solution(mesh):
    return jax.shard_map(
        local,
        mesh=mesh,
        in_specs=(
            P(("dp", "ctx"), None),
            P(("dp", "ctx"), None),
            P(("dp", "ctx"), None),
            P(("dp", "ctx"), None),
            P(("dp", "ctx"), None),
            P(("dp", "ctx"), None),
            P(),
            P(),
            P(),
            P("dp", None),
            P("dp"),
        ),
        out_specs=(
            P(("dp", "ctx"), None),
            P(("dp", "ctx"), None),
            P(("dp", "ctx"), None),
            P(("dp", "ctx"), None),
            P(("dp", "ctx"), None),
        ),
        check_vma=False,
    )
```

profile of v0, /device:TPU:0, one launch (start us, length us, event | category | flops | bytes accessed | tf_op | source)
XLA Modules:
  0.0 698.5 jit_solution(627785856243509264)
XLA Ops:
  9.4 6.4 all-to-all-start
  15.7 4.1 copy.259
  21.5 4.5 all-to-all-start.1
  27.4 11.1 %psum.7 = f32[]{:T(128)} all-reduce(f32[]{:T(128)} %bitcast.55), channel_id=1, replica_groups=mesh['dp'=4,'ctx'=8] {'dp'}, use_global_device_ids=true, to_apply=%region_0.0 | all-reduce | flops 1 | bytes 8 | tf_op jit(solution)/shard_map/psum | solution.py:192
  38.7 4.1 copy.260
  52.2 4.6 exponential_select_fusion
  57.7 22.9 %all-gather.5.cloned.1.call-done = bf16[1024,512]{1,0:T(8,128)(2,1)} async-done(((bf16[128,512]{1,0:T(8,128)(2,1)}), bf16[1024,512]{1,0:T(8,128)(2,1)}) %all-gather.5.cloned.1.call-update) | async-done | bytes 1048592 | tf_op jit(solution)/shard_map/all_gather | solution.py:205
  82.3 3.8 all-to-all-done.1
  86.1 4.4 all-to-all-start.2
  92.4 4.4 fusion.63
  99.3 16.2 %while.47 = (s32[]{:T(128)}, f32[1,16,64,128]{3,2,1,0:T(8,128)S(1)}, f32[8,1,16,64,128]{4,3,2,1,0:T(8,128)}, f32[8,1,16]{2,1,0:T(1,128)S(1)}, f32[8,1,16,64,128]...) while((s32[]{:T(128)}, f32[1,16,64,128]{3,2,1,0:T(8,128)S(1)}, ...), condition=%wide.region_8.9_spmd.clone, body=%wide.region_7.8_spmd.clone.sunk | while | flops 524292 | bytes 2621752 | solution.py:111
  115.5 23.9 %all-to-all-done.2 = bf16[128,8,1024]{0,2,1:T(8,128)(2,1)} async-done(((bf16[128,8,1024]{0,2,1:T(8,128)(2,1)}), bf16[128,8,1024]{0,2,1:T(8,128)(2,1)}, u32[]{:S(2)}, u32[]{:S(2)}) %all-to-all-start.2) | async-done | bytes 2097184 | tf_op jit(solution)/shard_map/all_to_all | solution.py:198
  141.4 3.5 fusion.66
  147.4 16.3 %while.48 = (s32[]{:T(128)}, f32[1,16,64,128]{3,2,1,0:T(8,128)S(1)}, f32[8,1,16,64,128]{4,3,2,1,0:T(8,128)}, f32[8,1,16]{2,1,0:T(1,128)S(1)}, f32[8,1,16,64,128]{4,3,2,1,0:T(8,128)}, /*index=5*/s32[]{:T(128)}, s32[]{:T(128)}) while((s32[]{:T(128)}, f32[1,16,64,128]{3,2,1,0:T(8,128)S(1)}, f32[8,1,16,64,128]{4,3,2,1,0:T(8,128)}, ...), condition=%wide.region_6.7_spmd.clone, body=%wide.region_5.6_spmd.clone.sunk | while | flops 524291 | bytes 2622240 | solution.py:102
  163.7 277.8 %while.46 = (s32[]{:T(128)}, bf16[8,128,1,16,64]{1,4,3,2,0:T(8,128)(2,1)}, f32[8,128,1,128]{3,1,0,2:T(8,128)}, f32[8,128,1,128]{3,1,0,2:T(8,128)}, bf16[8,128,1,...) while((s32[]{:T(128)}, ...), condition=%wide.region_19.20_spmd, body=%wide.region_9.19_spmd.sunk | while | flops 1300801536 | bytes 25205568 | solution.py:153
  199.4 3.4 broadcast_multiply_fusion.3
  234.2 3.4 broadcast_multiply_fusion.3
  447.5 8.2 %all_to_all.71 = bf16[8,128,16]{1,2,0:T(8,128)(2,1)S(1)} all-to-all(bf16[8,128,16]{1,2,0:T(8,128)(2,1)S(1)} %bitcast.431), channel_id=1, replica_groups=mesh['dp'=4,'ctx'=8] {'ctx'}, dimensions={0} | all-to-all | bytes 65536 | tf_op jit(solution)/shard_map/all_to_all | solution.py:240
  458.3 3.9 copy.241
  462.3 4.4 all-to-all-start.3
  467.4 69.0 %all-to-all-done.3 = bf16[8,128,1024]{2,1,0:T(8,128)(2,1)} async-done(((bf16[8,128,1024]{2,1,0:T(8,128)(2,1)}), bf16[8,128,1024]{2,1,0:T(8,128)(2,1)}, u32[]{:S(2)}, u32[]{:S(2)}) %all-to-all-start.3) | async-done | bytes 2097184 | tf_op jit(solution)/shard_map/all_to_all | solution.py:233
  536.4 3.9 copy.242
  540.3 4.1 copy.246
  547.6 142.7 %reduce-scatter.8.cloned.1.call-done = f32[256,128]{0,1:T(8,128)} async-done(((f32[8192,128]{0,1:T(8,128)}), f32[256,128]{0,1:T(8,128)}) %reduce-scatter.8.cloned.1.call-update) | async-done | bytes 131088 | tf_op jit(solution)/shard_map/reduce_scatter | solution.py:259
  (485 shorter events, 341.5 us)
Async XLA Ops:
  7.2 448.5 %copy-start = (bf16[128,8192]{1,0:T(8,128)(2,1)S(1)}, bf16[128,8192]{1,0:T(8,128)(2,1)}, u32[]{:S(2)}) copy-start(bf16[128,8192]{1,0:T(8,128)(2,1)} %param.22) | copy-start | bytes 6291460
  7.2 49.6 %all-gather.3.cloned.1.call-start = ((), (), s32[]{:S(2)}) async-start(), calls=%async_computation.8 | async-start | bytes 1179648 | tf_op jit(solution)/shard_map/all_gather | solution.py:206
  9.4 12.1 %all-to-all-start = ((bf16[128,8,16]{0,2,1:T(8,128)(2,1)}), bf16[128,8,16]{0,2,1:T(8,128)(2,1)S(1)}, u32[]{:S(2)}, u32[]{:S(2)}) async-start(bf16[128,8,16]{0,2,1:T(8,128)(2,1)} %bitcast.49), calls=%async_computation | async-start | bytes 65536 | tf_op jit(solution)/shard_map/all_to_all | solution.py:200
  15.7 22.7 %copy-start.10 = (s32[1,4]{1,0:T(1,128)S(1)}, s32[1,4]{1,0:T(1,128)}, u32[]{:S(2)}) copy-start(s32[1,4]{1,0:T(1,128)} %param.26) | copy-start | bytes 52
  21.5 21.3 %copy-start.8 = (f32[128]{0:T(128)S(1)}, f32[128]{0:T(128)}, u32[]{:S(2)}) copy-start(f32[128]{0:T(128)} %param.24) | copy-start | bytes 1540
  21.5 21.4 %copy-start.9 = (f32[128]{0:T(128)S(1)}, f32[128]{0:T(128)}, u32[]{:S(2)}) copy-start(f32[128]{0:T(128)} %param.25) | copy-start | bytes 1540
  21.5 23.5 %copy-start.11 = (f32[128]{0:T(128)S(1)}, f32[128]{0:T(128)}, u32[]{:S(2)}) copy-start(f32[128]{0:T(128)} %param.23) | copy-start | bytes 1540
  21.5 64.6 %all-to-all-start.1 = ((bf16[128,8,1024]{0,2,1:T(8,128)(2,1)}), bf16[128,8,1024]{0,2,1:T(8,128)(2,1)}, u32[]{:S(2)}, u32[]{:S(2)}) async-start(bf16[128,8,1024]{0,2,1:T(8,128)(2,1)} %bitcast.408), calls=%async_computation.1 | async-start | bytes 4194304 | tf_op jit(solution)/shard_map/all_to_all | solution.py:199
  26.0 54.6 %all-gather.5.cloned.1.call-start = ((), (), s32[]{:S(2)}) async-start(), calls=%async_computation.9 | async-start | bytes 1179648 | tf_op jit(solution)/shard_map/all_gather | solution.py:205
  86.1 53.4 %all-to-all-start.2 = ((bf16[128,8,1024]{0,2,1:T(8,128)(2,1)}), bf16[128,8,1024]{0,2,1:T(8,128)(2,1)}, u32[]{:S(2)}, u32[]{:S(2)}) async-start(bf16[128,8,1024]{0,2,1:T(8,128)(2,1)} %bitcast.409), calls=%async_computation.2 | async-start | bytes 4194304 | tf_op jit(solution)/shard_map/all_to_all | solution.py:198
  90.4 453.9 %reduce-scatter.4.cloned.1.call-start = ((), (), s32[]{:S(2)}) async-start(), calls=%async_computation.10 | async-start | bytes 2359296 | tf_op jit(solution)/shard_map/reduce_scatter | solution.py:252
  115.5 25.9 %copy-start.3 = (bf16[1024,128]{1,0:T(8,128)(2,1)S(1)}, bf16[1024,128]{1,0:T(8,128)(2,1)}, u32[]{:S(2)}) copy-start(bf16[1024,128]{1,0:T(8,128)(2,1)} %constant_dynamic-slice_fusion.5) | copy-start | bytes 786436
  115.5 25.9 %copy-start.5 = (f32[8,128,16]{1,2,0:T(8,128)S(1)}, f32[8,128,16]{1,2,0:T(8,128)}, u32[]{:S(2)}) copy-start(f32[8,128,16]{1,2,0:T(8,128)} %get-tuple-element.559) | copy-start | bytes 196612
  179.0 16.3 %copy-start.4 = (bf16[1024,128]{1,0:T(8,128)(2,1)S(1)}, bf16[1024,128]{1,0:T(8,128)(2,1)}, u32[]{:S(2)}) copy-start(bf16[1024,128]{1,0:T(8,128)(2,1)} %get-tuple-element.909) | copy-start | bytes 786436 | tf_op jit(solution)/shard_map/while
  213.7 16.4 %copy-start.4 = (bf16[1024,128]{1,0:T(8,128)(2,1)S(1)}, bf16[1024,128]{1,0:T(8,128)(2,1)}, u32[]{:S(2)}) copy-start(bf16[1024,128]{1,0:T(8,128)(2,1)} %get-tuple-element.909) | copy-start | bytes 786436 | tf_op jit(solution)/shard_map/while
  248.5 16.3 %copy-start.4 = (bf16[1024,128]{1,0:T(8,128)(2,1)S(1)}, bf16[1024,128]{1,0:T(8,128)(2,1)}, u32[]{:S(2)}) copy-start(bf16[1024,128]{1,0:T(8,128)(2,1)} %get-tuple-element.909) | copy-start | bytes 786436 | tf_op jit(solution)/shard_map/while
  283.1 16.3 %copy-start.4 = (bf16[1024,128]{1,0:T(8,128)(2,1)S(1)}, bf16[1024,128]{1,0:T(8,128)(2,1)}, u32[]{:S(2)}) copy-start(bf16[1024,128]{1,0:T(8,128)(2,1)} %get-tuple-element.909) | copy-start | bytes 786436 | tf_op jit(solution)/shard_map/while
  317.8 16.3 %copy-start.4 = (bf16[1024,128]{1,0:T(8,128)(2,1)S(1)}, bf16[1024,128]{1,0:T(8,128)(2,1)}, u32[]{:S(2)}) copy-start(bf16[1024,128]{1,0:T(8,128)(2,1)} %get-tuple-element.909) | copy-start | bytes 786436 | tf_op jit(solution)/shard_map/while
  352.5 16.3 %copy-start.4 = (bf16[1024,128]{1,0:T(8,128)(2,1)S(1)}, bf16[1024,128]{1,0:T(8,128)(2,1)}, u32[]{:S(2)}) copy-start(bf16[1024,128]{1,0:T(8,128)(2,1)} %get-tuple-element.909) | copy-start | bytes 786436 | tf_op jit(solution)/shard_map/while
  387.2 16.3 %copy-start.4 = (bf16[1024,128]{1,0:T(8,128)(2,1)S(1)}, bf16[1024,128]{1,0:T(8,128)(2,1)}, u32[]{:S(2)}) copy-start(bf16[1024,128]{1,0:T(8,128)(2,1)} %get-tuple-element.909) | copy-start | bytes 786436 | tf_op jit(solution)/shard_map/while
  421.9 16.3 %copy-start.4 = (bf16[1024,128]{1,0:T(8,128)(2,1)S(1)}, bf16[1024,128]{1,0:T(8,128)(2,1)}, u32[]{:S(2)}) copy-start(bf16[1024,128]{1,0:T(8,128)(2,1)} %get-tuple-element.909) | copy-start | bytes 786436 | tf_op jit(solution)/shard_map/while
  446.8 99.2 %reduce-scatter.6.cloned.1.call-start = ((), (), s32[]{:S(2)}) async-start(), calls=%async_computation.11 | async-start | bytes 2359296 | tf_op jit(solution)/shard_map/reduce_scatter | solution.py:253
  447.4 243.0 %reduce-scatter.8.cloned.1.call-start = ((), (), s32[]{:S(2)}) async-start(), calls=%async_computation.12 | async-start | bytes 4325376 | tf_op jit(solution)/shard_map/reduce_scatter | solution.py:259
  462.3 74.1 %all-to-all-start.3 = ((bf16[8,128,1024]{2,1,0:T(8,128)(2,1)}), bf16[8,128,1024]{2,1,0:T(8,128)(2,1)}, u32[]{:S(2)}, u32[]{:S(2)}) async-start(bf16[8,128,1024]{2,1,0:T(8,128)(2,1)} %copy.241), calls=%async_computation.3 | async-start | bytes 4194304 | tf_op jit(solution)/shard_map/all_to_all | solution.py:233
  (4 other events, 11.5 us)
Sparse Core Ops, SparseCore 0:
  9.6 28.6 all-gather.2
  39.8 40.7 all-gather.4
  446.9 40.2 reduce-scatter.3
  489.4 52.6 reduce-scatter.5
  544.2 146.0 reduce-scatter.7
where the time goes:
time: 706 us; the launch traced here: 699 us
  waiting for transfers between devices  266 us (38%)
  matrix products  137 us (19%)
  local copies, waits for them, and re-layouts  130 us (18%)
  other arithmetic  110 us (16%)
  starting transfers between devices  19.8 us (3%)
  blocking collectives  19.2 us (3%)
  between operations  15.3 us (2%)
    reduce_scatter x1, waiting for transfers between devices, local(): lax.psum_scatter(jnp.einsum('td,th->dh', hidden, grad_raw, preferred_elem...  143 us
    all_to_all x1, waiting for transfers between devices, local(): lax.all_to_all(grad_values.reshape(length, local_heads * P_SIZE).astype(j...  69 us
    dot_general x8, matrix products, block_grads(): jnp.einsum('ugkp,sgkp->gkus', cotangent, values, precision=HIGHEST)  26.9 us
    dot_general x8, matrix products, block_grads(): jnp.einsum('gkus,ugkp->sgkp', coupled, cotangent, precision=HIGHEST)  26.6 us
    dot_general x8, matrix products, block_grads(): jnp.einsum('sgkp,gkpn->sgkn', values, flow_in, precision=HIGHEST)  24.3 us
    all_to_all x1, waiting for transfers between devices, local(): lax.all_to_all(inputs, 'ctx', split_axis=1, concat_axis=0, tiled=True)  23.9 us
    all_gather x1, waiting for transfers between devices, local(): lax.all_gather(b_matrix, 'ctx', axis=0, tiled=True)  22.9 us
    another operation x8, local copies, waits for them, and re-layouts, block_grads(): crossing = jnp.cumsum(products, axis=-1) - products  20.9 us
  transfers between devices with their start and end apart: 9, of which 6 were waited for; matrix products, arithmetic and copies ran while one was open for 10% of the time, Pallas kernels for 0%

commit v1 on v0

v1 whole, which is shorter than its diff:
```python
import functools
import math

import jax
import jax.numpy as jnp
from jax import lax
from jax.experimental import pallas as pl
from jax.experimental.pallas import tpu as pltpu
from jax.sharding import PartitionSpec as P

HEAD = 64
N = 128
Q = 128
LANES = 128
WIDE1 = 1024
WIDE2 = 512
WIDE3 = 1024
CHUNKS = 2
F32 = jnp.float32
BF16 = jnp.bfloat16
HIGHEST = lax.Precision.HIGHEST


def split(value):
    high = value.astype(BF16)
    return high, (value - high.astype(F32)).astype(BF16)


def nn(a, b):
    return lax.dot_general(a, b, (((1,), (0,)), ((), ())), preferred_element_type=F32)


def nt(a, b):
    return lax.dot_general(a, b, (((1,), (1,)), ((), ())), preferred_element_type=F32)


def tn(a, b):
    return lax.dot_general(a, b, (((0,), (0,)), ((), ())), preferred_element_type=F32)


def iota(shape, axis):
    return lax.broadcasted_iota(jnp.int32, shape, axis)


def head_selector(first_head, width):
    shape = (LANES, width)
    return ((iota(shape, 1) // HEAD + first_head) == iota(shape, 0)).astype(F32).astype(BF16)


def forward_role(shape):
    return iota(shape, 0) < (lax.axis_index("ctx") % 2) * (1 << 20)


def prep_kernel(
    docs_ref, raw_ref, far_ref, rate_ref, bias_ref, skip_ref,
    whi_ref, wlo_ref, fhi_ref, flo_ref, col_ref, row_ref, mask_ref, khi_ref, klo_ref, ratio_ref, rate_out_ref, down_ref,
):
    ctx = lax.axis_index("ctx")
    core = ctx % 2
    square = (Q, Q)
    sub, lane = iota(square, 0), iota(square, 1)
    lower = (sub >= lane).astype(F32)
    neg = -jnp.exp(rate_ref[...])
    bias = bias_ref[...]
    starts, total = [], jnp.int32(0)
    for d in range(docs_ref.shape[1]):
        starts.append(total)
        total = total + docs_ref[0, d]

    def segments(base, index):
        seg, last = jnp.zeros(square, jnp.int32), jnp.int32(0)
        for start in starts:
            rel = jnp.where(start >= base, start - base, 1 << 20)
            seg = seg + (index >= rel).astype(jnp.int32)
            last = last + jnp.where(rel < Q, 1, 0)
        return seg, last

    def side(raw, base):
        shifted = raw.astype(F32) + bias
        step = jnp.maximum(shifted, 0.0) + jnp.log1p(jnp.exp(-jnp.abs(shifted)))
        summed = jnp.dot(lower, step * neg, precision=HIGHEST, preferred_element_type=F32)
        seg, last = segments(base, sub)
        before = jnp.where(seg == 0, jnp.exp(summed), 0.0)
        behind = jnp.where(seg == last, jnp.exp(summed[Q - 1 :, :] - summed), 0.0)
        return shifted, step, summed, seg, before, behind

    own_base, far_base = ctx * Q, (ctx + 1 - 2 * core) * Q
    shifted, step, summed, seg, before, behind = side(raw_ref[...], own_base)
    _, step_f, _, _, before_f, behind_f = side(far_ref[...], far_base)
    down, down_f = before[Q - 1 :, :], before_f[Q - 1 :, :]
    forward = forward_role(square)
    own = jnp.where(forward, behind * step, before)
    far = jnp.where(forward, behind_f * step_f, before_f)
    row = iota((16, LANES), 0)
    rows = jnp.where(row == 0, down_f, jnp.where(row == 1, down * down_f, jnp.where(row == 2, skip_ref[...], 0.0)))
    whi_ref[...], wlo_ref[...] = split(jnp.concatenate([own, far * down, rows], axis=0))
    fhi_ref[...], flo_ref[...] = split(far)
    col_ref[...] = summed - jnp.log(jnp.maximum(step, 1e-37))
    row_ref[...] = summed.T
    seg_u, _ = segments(own_base, lane)
    mask_ref[...] = jnp.where((lane >= sub) & (seg_u == seg), 0.0, -1e30)
    khi_ref[...], klo_ref[...] = split(jnp.concatenate([step * behind, before], axis=0))
    sigmoid = 1.0 / (1.0 + jnp.exp(-shifted))
    ratio_ref[...] = jnp.where(step < 1e-30, 1.0, sigmoid / jnp.maximum(step, 1e-30))
    rate_out_ref[...] = neg * sigmoid
    down_ref[...] = jnp.broadcast_to(down, (8, LANES))


def prep(docs, raw, far_small, rate, bias, skip, far_block):
    full = lambda shape: pl.BlockSpec(shape, lambda i: (0, 0))
    sq = jax.ShapeDtypeStruct((Q, LANES), F32)
    outs = [
        jax.ShapeDtypeStruct((2 * Q + 16, LANES), BF16),
        jax.ShapeDtypeStruct((2 * Q + 16, LANES), BF16),
        jax.ShapeDtypeStruct((Q, LANES), BF16),
        jax.ShapeDtypeStruct((Q, LANES), BF16),
        sq, sq, sq,
        jax.ShapeDtypeStruct((2 * Q, LANES), BF16),
        jax.ShapeDtypeStruct((2 * Q, LANES), BF16),
        sq, sq,
        jax.ShapeDtypeStruct((8, LANES), F32),
    ]
    return pl.pallas_call(
        prep_kernel,
        name="prep",
        grid=(1,),
        in_specs=[
            pl.BlockSpec(memory_space=pltpu.SMEM),
            full((Q, LANES)),
            pl.BlockSpec((Q, LANES), lambda i: (0, far_block)),
            full((1, LANES)), full((1, LANES)), full((1, LANES)),
        ],
        out_specs=[full(o.shape) for o in outs],
        out_shape=outs,
        cost_estimate=pl.CostEstimate(flops=20_000_000, transcendentals=200_000, bytes_accessed=1_000_000),
    )(docs, raw, far_small, rate, bias, skip)


def state_kernel(first, whi_ref, wlo_ref, x_ref, g_ref, far_ref, b_ref, c_ref, mf_ref, t_ref, rows_ref):
    i = pl.program_id(0)
    sel = head_selector((first + i) * (WIDE1 // HEAD), WIDE1)
    wide = nn(whi_ref[...], sel) + nn(wlo_ref[...], sel)
    forward = forward_role((Q, WIDE1))
    own = jnp.where(forward, x_ref[...].astype(F32), g_ref[...].astype(F32))
    scaled = jnp.concatenate([own * wide[:Q], far_ref[...].astype(F32) * wide[Q : 2 * Q]], axis=0)
    high, low = split(scaled)
    role = forward_role((Q, N))
    m_own = jnp.where(role, b_ref[...].astype(F32), c_ref[...].astype(F32))
    m = jnp.concatenate([m_own, mf_ref[...].astype(F32)], axis=0).T.astype(BF16)
    t_ref[...] = (nn(m, high) + nn(m, low)).astype(BF16)
    rows_ref[...] = wide[2 * Q :]


def chip_state(chunk, width, group_width, whi, wlo, x, g, far, b, c, far_small):
    steps = width // WIDE1
    first = chunk * steps
    group = lambda i: (first + i) * WIDE1 // group_width
    whole = lambda a: pl.BlockSpec(a.shape, lambda i: (0, 0))
    return pl.pallas_call(
        functools.partial(state_kernel, first),
        name="chip_state",
        grid=(steps,),
        in_specs=[
            whole(whi), whole(wlo),
            pl.BlockSpec((Q, WIDE1), lambda i: (0, first + i)),
            pl.BlockSpec((Q, WIDE1), lambda i: (0, first + i)),
            pl.BlockSpec((Q, WIDE1), lambda i: (0, i)),
            pl.BlockSpec((Q, N), lambda i: (0, group(i))),
            pl.BlockSpec((Q, N), lambda i: (0, group(i))),
            pl.BlockSpec((Q, N), lambda i: (0, group(i))),
        ],
        out_specs=[pl.BlockSpec((N, WIDE1), lambda i: (0, i)), pl.BlockSpec((16, WIDE1), lambda i: (0, i))],
        out_shape=[jax.ShapeDtypeStruct((N, width), BF16), jax.ShapeDtypeStruct((16, width), F32)],
        cost_estimate=pl.CostEstimate(flops=8 * N * 2 * Q * width, transcendentals=0, bytes_accessed=8 * Q * width),
    )(whi, wlo, x, g, far, b, c, far_small)


def block_kernel(
    first, per_group, fhi_ref, flo_ref, col_ref, row_ref, mask_ref, rows_ref, x_ref, g_ref, far_ref, b_ref, c_ref, mf_ref,
    p_ref, tf_ref, cc_ref, r_ref, gb_ref, gc_ref, cross_ref, w_ref, rt_ref,
):
    i = pl.program_id(0)
    heads = WIDE2 // HEAD
    block = first + i

    @pl.when(i == 0)
    def _():
        cc_ref[...] = jnp.zeros_like(cc_ref)
        rt_ref[...] = jnp.zeros_like(rt_ref)

    @pl.when(i % per_group == 0)
    def _():
        cross = nt(b_ref[...], c_ref[...])
        cross_ref[...] = jnp.concatenate([cross, cross], axis=1)
        w_ref[...] = jnp.zeros_like(w_ref)

    lane = iota((Q, LANES), 1)
    left = (lane < HEAD).astype(F32).astype(BF16)
    right = (lane >= HEAD).astype(F32).astype(BF16)
    mask = mask_ref[...]
    cross = cross_ref[...]
    cols = pltpu.roll(col_ref[...], (LANES - heads * block) % LANES, 1)
    srow = row_ref[pl.ds(pl.multiple_of(heads * block, 8), heads), :]
    skip = rows_ref[2:3, :]
    cc = jnp.zeros((Q, LANES), F32)
    wsum = w_ref[...]
    sums = []
    for j in range(heads // 2):
        at = slice(LANES * j, LANES * (j + 1))
        xp, gp = x_ref[:, at], g_ref[:, at]
        stacked = jnp.concatenate([gp * left, gp * right], axis=0)
        pair = nt(xp, stacked)
        gap = jnp.concatenate(
            [mask + (srow[k : k + 1, :] - cols[:, k : k + 1]) for k in (2 * j, 2 * j + 1)], axis=1
        )
        within = jnp.exp(gap)
        coupled = within * cross
        weighted = within * pair
        product = coupled * pair
        wsum = wsum + weighted
        high, low = split(coupled)
        p_ref[:, at] = nn(high, stacked) + nn(low, stacked) + skip[:, at] * gp.astype(F32)
        over = jnp.sum(product, axis=0, keepdims=True)
        sums += [over[:, :Q], over[:, Q:]]
        for k in (0, 1):
            column = jnp.sum(product[:, Q * k : Q * (k + 1)], axis=1, keepdims=True)
            cc = jnp.where(lane == heads * block + 2 * j + k, column, cc)
    cc_ref[...] += cc
    rt_ref[pl.ds(pl.multiple_of(heads * block, 8), heads), :] = jnp.concatenate(sums, axis=0)
    w_ref[...] = wsum

    sel = head_selector(block * heads, WIDE2)
    wide = nn(fhi_ref[...], sel) + nn(flo_ref[...], sel)
    high, low = split(far_ref[...].astype(F32) * wide)
    m = mf_ref[...].astype(F32).T.astype(BF16)
    tf_ref[...] = nn(m, high) + nn(m, low)

    @pl.when(i % per_group == per_group - 1)
    def _():
        folded = wsum[:, :Q] + wsum[:, Q:]
        high, low = split(folded)
        gb_ref[...] = nn(high, c_ref[...]) + nn(low, c_ref[...])
        high, low = split(folded.T)
        gc_ref[...] = nn(high, b_ref[...]) + nn(low, b_ref[...])

    @pl.when(i == pl.num_programs(0) - 1)
    def _():
        r_ref[...] = rt_ref[...].T


def within_block(chunk, width, group_width, fhi, flo, col, row, mask, rows, x, g, far, b, c, far_small):
    steps = width // WIDE2
    first = chunk * steps
    per_group = group_width // WIDE2
    whole = lambda a: pl.BlockSpec(a.shape, lambda i: (0, 0))
    group = pl.BlockSpec((Q, N), lambda i: (0, (first + i) // per_group))
    groups = width // group_width
    return pl.pallas_call(
        functools.partial(block_kernel, first, per_group),
        name="within_block",
        grid=(steps,),
        in_specs=[
            whole(fhi), whole(flo), whole(col), whole(row), whole(mask),
            pl.BlockSpec((16, WIDE2), lambda i: (0, i)),
            pl.BlockSpec((Q, WIDE2), lambda i: (0, first + i)),
            pl.BlockSpec((Q, WIDE2), lambda i: (0, first + i)),
            pl.BlockSpec((Q, WIDE2), lambda i: (0, i)),
            group, group, group,
        ],
        out_specs=[
            pl.BlockSpec((Q, WIDE2), lambda i: (0, i)),
            pl.BlockSpec((N, WIDE2), lambda i: (0, i)),
            pl.BlockSpec((Q, LANES), lambda i: (0, 0)),
            pl.BlockSpec((Q, LANES), lambda i: (0, 0)),
            pl.BlockSpec((Q, N), lambda i: (0, i // per_group)),
            pl.BlockSpec((Q, N), lambda i: (0, i // per_group)),
        ],
        out_shape=[
            jax.ShapeDtypeStruct((Q, width), F32),
            jax.ShapeDtypeStruct((N, width), F32),
            jax.ShapeDtypeStruct((Q, LANES), F32),
            jax.ShapeDtypeStruct((Q, LANES), F32),
            jax.ShapeDtypeStruct((Q, groups * N), F32),
            jax.ShapeDtypeStruct((Q, groups * N), F32),
        ],
        scratch_shapes=[pltpu.VMEM((Q, 2 * Q), F32), pltpu.VMEM((Q, 2 * Q), F32), pltpu.VMEM((LANES, Q), F32)],
        cost_estimate=pl.CostEstimate(
            flops=16 * Q * Q * width, transcendentals=Q * Q * width // HEAD, bytes_accessed=14 * Q * width
        ),
    )(fhi, flo, col, row, mask, rows, x, g, far, b, c, far_small)


def finish_kernel(
    first, per_group, stages, last_ctx, weight_ref, khi_ref, klo_ref, ratio_ref, rate_ref, down_ref, cc_ref, r_ref, prev_ref, rows_ref,
    x_ref, g_ref, p_ref, tf_ref, b_ref, c_ref, gbi_ref, gci_ref, *refs,
):
    own_refs, other_refs = refs[:stages], refs[stages : 2 * stages]
    gi_ref, gb_ref, gc_ref, gs_ref, acc_ref, ab_ref, ac_ref = refs[-7:]
    i = pl.program_id(0)
    ctx = lax.axis_index("ctx")
    core = ctx % 2
    chip = ctx // 2
    low_edge = jnp.where(chip == 0, 0, 1)
    high_edge = jnp.where(chip == last_ctx // 2, 0, 1)
    weight = weight_ref[0, 0]

    @pl.when(i == 0)
    def _():
        acc_ref[...] = jnp.zeros_like(acc_ref)

    @pl.when(i % per_group == 0)
    def _():
        ab_ref[...] = jnp.zeros_like(ab_ref)
        ac_ref[...] = jnp.zeros_like(ac_ref)

    sel = head_selector((first + i) * (WIDE3 // HEAD), WIDE3)
    wide = nn(khi_ref[...], sel) + nn(klo_ref[...], sel)
    behind, before = wide[:Q], wide[Q:]
    shape = (N, WIDE3)
    sub = iota(shape, 0)
    carried, other = own_refs[0][...].astype(F32), other_refs[0][...].astype(F32)
    for k in range(1, stages):
        carried = carried + own_refs[k][...].astype(F32)
        other = other + other_refs[k][...].astype(F32)
    own_edge = jnp.where(core == 1, low_edge, high_edge)
    other_edge = jnp.where(core == 1, high_edge, low_edge)
    carried = jnp.where(sub < own_edge * N, carried, 0.0)
    other = jnp.where(sub < other_edge * N, other, 0.0)
    own = tf_ref[...] + rows_ref[0:1, :] * carried
    forward = forward_role(shape)
    state = jnp.where(forward, own, other)
    flow = jnp.where(forward, other, own)
    state_h, state_l = split(state)
    flow_h, flow_l = split(flow)
    b, c = b_ref[...], c_ref[...]
    x = x_ref[...].astype(F32)
    g = g_ref[...].astype(F32) * before
    reached = behind * (nn(b, flow_h) + nn(b, flow_l))
    gi_ref[...] = (weight * (p_ref[...] + reached)).astype(BF16)
    entered = g * (nn(c, state_h) + nn(c, state_l))
    g_h, g_l = split(g)
    x_h, x_l = split(x * behind)
    ab_ref[...] += nt(x_h, flow_h) + nt(x_h, flow_l) + nt(x_l, flow_h)
    ac_ref[...] += nt(g_h, state_h) + nt(g_h, state_l) + nt(g_l, state_h)
    through = jnp.sum((state * flow).reshape(N // 16, 16, WIDE3), axis=0)
    red_h, red_l = split(jnp.concatenate([x * reached, entered, through], axis=0))
    acc_ref[...] += nt(red_h, sel) + nt(red_l, sel)

    @pl.when(i % per_group == per_group - 1)
    def _():
        gb_ref[...] = (weight * (gbi_ref[...] + ab_ref[...])).astype(BF16)
        gc_ref[...] = (weight * (gci_ref[...] + ac_ref[...])).astype(BF16)

    @pl.when(i == pl.num_programs(0) - 1)
    def _():
        leaving, entering = acc_ref[:Q, :], acc_ref[Q : 2 * Q, :]
        passing = jnp.sum(acc_ref[2 * Q :, :], axis=0, keepdims=True) * down_ref[0:1, :]
        upper = (iota((Q, Q), 0) <= iota((Q, Q), 1)).astype(F32)
        inside = r_ref[...] + entering - cc_ref[...] - leaving
        decay = jnp.dot(upper, inside, precision=HIGHEST, preferred_element_type=F32)
        decay = decay + (passing + jnp.sum(leaving, axis=0, keepdims=True))
        steps = (cc_ref[...] + leaving) * ratio_ref[...] + rate_ref[...] * decay
        gs_ref[...] = prev_ref[...] + weight * steps


def finish(chunk, width, group_width, last_ctx, weight, tables, cc, r, prev, rows, x, g, p, tf, b, c, gbi, gci, own, other, partial):
    khi, klo, ratio, rate, down = tables
    steps = width // WIDE3
    first = chunk * steps
    per_group = group_width // WIDE3
    stages = len(own)
    whole = lambda a: pl.BlockSpec(a.shape, lambda i: (0, 0))
    local = pl.BlockSpec((Q, WIDE3), lambda i: (0, i))
    spread = pl.BlockSpec((Q, WIDE3), lambda i: (0, first + i))
    group = pl.BlockSpec((Q, N), lambda i: (0, (first + i) // per_group))
    inner = pl.BlockSpec((Q, N), lambda i: (0, i // per_group))
    operands = [weight, khi, klo, ratio, rate, down, cc, r, prev, rows, x, g, p, tf, b, c, gbi, gci, *own, *other]
    specs = [
        pl.BlockSpec(memory_space=pltpu.SMEM),
        whole(khi), whole(klo), whole(ratio), whole(rate), whole(down), whole(cc), whole(r), whole(prev),
        pl.BlockSpec((16, WIDE3), lambda i: (0, i)),
        spread, spread, local, local, group, group, inner, inner,
    ] + [local] * (2 * stages)
    aliases = {}
    if partial is not None:
        aliases = {len(operands) + k: k for k in range(3)}
        operands += list(partial)
        specs += [pl.BlockSpec(memory_space=pl.ANY)] * 3
    return pl.pallas_call(
        functools.partial(finish_kernel, first, per_group, stages, last_ctx),
        name="finish",
        grid=(steps,),
        in_specs=specs,
        out_specs=[spread, group, group, pl.BlockSpec((Q, LANES), lambda i: (0, 0))],
        out_shape=[
            jax.ShapeDtypeStruct(x.shape, BF16),
            jax.ShapeDtypeStruct(b.shape, BF16),
            jax.ShapeDtypeStruct(c.shape, BF16),
            jax.ShapeDtypeStruct((Q, LANES), F32),
        ],
        scratch_shapes=[pltpu.VMEM((2 * Q + 16, LANES), F32), pltpu.VMEM((Q, N), F32), pltpu.VMEM((Q, N), F32)],
        input_output_aliases=aliases,
        cost_estimate=pl.CostEstimate(flops=24 * N * Q * width, transcendentals=0, bytes_accessed=20 * Q * width),
    )(*operands)


def local(inputs, out_grad, b_matrix, c_matrix, step_raw, hidden, log_rates, step_bias, skip_head_gain, doc_lengths, counts):
    ctx_size, dp_size = lax.axis_size("ctx"), lax.axis_size("dp")
    chips = ctx_size // 2
    tokens, model = inputs.shape
    groups = b_matrix.shape[1] // N
    group_width = model // groups
    width = model // CHUNKS
    stages = max(1, chips // 2)
    ctx = lax.axis_index("ctx")
    dp = lax.axis_index("dp")
    core = ctx % 2
    chip = ctx // 2

    def swap(value):
        return lax.ppermute(value, "ctx", [(k, k ^ 1) for k in range(ctx_size)])

    chain_pairs = []
    for z in range(chips):
        chain_pairs.append((2 * z + 1, 2 * z + 3 if z < chips - 1 else 2 * z))
        chain_pairs.append((2 * z, 2 * z - 2 if z > 0 else 1))

    def chain(value):
        return lax.ppermute(value, "ctx", chain_pairs)

    def across(value, m):
        return lax.ppermute(value, "dp", [(k, k ^ m) for k in range(dp_size)])

    def along(value, m):
        return lax.ppermute(value, "ctx", [(k, k ^ (2 * m)) for k in range(ctx_size)])

    first_core = core == 0
    far_small = swap(jnp.concatenate([jnp.where(first_core, b_matrix, c_matrix), step_raw], axis=1))
    cuts = [slice(k * width, (k + 1) * width) for k in range(CHUNKS)]
    far = [swap(jnp.where(first_core, inputs[:, cut], out_grad[:, cut])) for cut in cuts]
    row = lambda a: a.reshape(1, -1)
    whi, wlo, fhi, flo, col, srow, mask, khi, klo, ratio, rate, down = prep(
        doc_lengths, step_raw, far_small, row(log_rates), row(step_bias), row(skip_head_gain), groups
    )
    formed = [
        chip_state(k, width, group_width, whi, wlo, inputs, out_grad, far[k], b_matrix, c_matrix, far_small)
        for k in range(CHUNKS)
    ]

    inner = jnp.where(first_core, chip < chips - 1, chip > 0)
    sending = [state for state, _ in formed]
    own = [[] for _ in range(CHUNKS)]
    other = [[] for _ in range(CHUNKS)]
    for stage in range(stages):
        for k in range(CHUNKS):
            arrived = chain(sending[k])
            own[k].append(arrived)
            other[k].append(swap(arrived))
            if stage < stages - 1:
                scale = formed[k][1][1:2, :]
                sending[k] = jnp.where(inner, arrived.astype(F32) * scale, 0.0).astype(BF16)

    count = counts.astype(F32)
    total = count
    m = 1
    while m < dp_size:
        total = total + across(total, m)
        m *= 2
    weight = (count * dp_size / total).reshape(1, 1)

    columns = model // dp_size
    cut_of = lambda index: lax.dynamic_slice_in_dim(hidden, index * columns, columns, 1)
    hidden_all = jnp.concatenate([cut_of(dp)] + [across(cut_of(dp ^ m), m) for m in range(1, dp_size)], axis=0)

    blocks = [
        within_block(
            k, width, group_width, fhi, flo, col, srow, mask, formed[k][1], inputs, out_grad, far[k], b_matrix, c_matrix, far_small
        )
        for k in range(CHUNKS)
    ]
    partial = None
    grad_steps = jnp.zeros((tokens, LANES), F32)
    for k in range(CHUNKS):
        p, tf, cc, r, gbi, gci = blocks[k]
        *partial, grad_steps = finish(
            k, width, group_width, ctx_size - 1, weight, (khi, klo, ratio, rate, down), cc, r, grad_steps, formed[k][1],
            inputs, out_grad, p, tf, b_matrix, c_matrix, gbi, gci, own[k], other[k], partial,
        )
    grad_inputs, grad_b, grad_c = partial
    grad_raw = grad_steps.astype(BF16)

    steps_all = jnp.concatenate([grad_raw] + [across(grad_raw, m) for m in range(1, dp_size)], axis=0)
    part = lax.dot_general(hidden_all, steps_all, (((0,), (0,)), ((), ())), preferred_element_type=F32)
    part = part.reshape(chips, 2, columns // ctx_size, LANES)
    pick = lambda index: lax.dynamic_index_in_dim(part, index, 1, keepdims=False)
    part = pick(core) + swap(pick(1 - core))
    piece = lambda index: lax.dynamic_index_in_dim(part, index, 0, keepdims=False)
    grad_weight = piece(chip)
    for m in range(1, chips):
        grad_weight = grad_weight + along(piece(chip ^ m), m)
    scaling = 1.0 / math.sqrt(dp_size * ctx_size * tokens)
    return (grad_inputs, grad_b, grad_c, grad_raw, grad_weight * scaling)


def solution(mesh):
    rows = P(("dp", "ctx"), None)
    return jax.shard_map(
        local,
        mesh=mesh,
        in_specs=(rows, rows, rows, rows, rows, rows, P(), P(), P(), P("dp", None), P("dp")),
        out_specs=(rows, rows, rows, rows, rows),
        check_vma=False,
    )
```

time: 706 us -> 154 us (0.22)
  waiting for transfers between devices: 266 us -> 54.5 us
  matrix products: 137 us -> 1.94 us
  local copies, waits for them, and re-layouts: 130 us -> 8.11 us
  other arithmetic: 110 us -> 5.87 us
  Pallas kernels: 0 us -> 56.9 us
  blocking collectives: 19.2 us -> 0 us
  between operations: 15.3 us -> 2.83 us
    reduce_scatter x3 -> x0, waiting for transfers between devices: 143 us -> none  [the longest x1 143 us: local(): lax.psum_scatter(jnp.einsum('td,th->dh', hidden, grad_raw, preferred_elem...]
    dot_general x75 -> x1, matrix products: 137 us -> 1.94 us  [local(): lax.dot_general(hidden_all, steps_all, (((0,), (0,)), ((), ())), preferre...]
    all_to_all x4 -> x0, waiting for transfers between devices: 98.4 us -> none  [the longest x1 69 us: local(): lax.all_to_all(grad_values.reshape(length, local_heads * P_SIZE).astype(j...]
    pallas_call x0 -> x7, Pallas kernels: none -> 56.9 us  [the longest x2 22.7 us: within_block(): pl.pallas_call(functools.partial(block_kernel, first, per_group), name='w...]
    ppermute x0 -> x23, waiting for transfers between devices: none -> 54.5 us  [the longest x4 36.3 us: chain(): return lax.ppermute(value, 'ctx', chain_pairs)]
    mul x52 -> x0, local copies, waits for them, and re-layouts: 33.1 us -> none  [the longest x8 11.5 us: block_grads(): products = weighted * cross_bc[:, None]]
    reduce_sum x24 -> x0, other arithmetic: 31.1 us -> none  [the longest x8 11.3 us: block_grads(): through = before[..., -1] * jnp.sum(flow_in * state_in, axis=(-2, -1))]
    another operation x11 -> x0, local copies, waits for them, and re-layouts: 27.1 us -> none  [the longest x8 20.9 us: block_grads(): crossing = jnp.cumsum(products, axis=-1) - products]
  transfers between devices with their start and end apart: 9 -> 23, of which waited for: 6 -> 12; matrix products, arithmetic and copies ran while one was open for 10% -> 4% of each run, Pallas kernels for 0% -> 37%
where the time goes in v1:
time: 154 us; the launch traced here: 153 us
  Pallas kernels  56.9 us (37%)
  waiting for transfers between devices  54.5 us (35%)
  starting transfers between devices  23.2 us (15%)
  local copies, waits for them, and re-layouts  8.11 us (5%)
  other arithmetic  5.87 us (4%)
  between operations  2.83 us (2%)
  matrix products  1.94 us (1%)
    ppermute x4, waiting for transfers between devices, chain(): return lax.ppermute(value, 'ctx', chain_pairs)  36.3 us
    pallas_call x2, Pallas kernels, within_block(): pl.pallas_call(functools.partial(block_kernel, first, per_group), name='w...  22.7 us
    pallas_call x2, Pallas kernels, finish(): pl.pallas_call(functools.partial(finish_kernel, first, per_group, stages,...  20.7 us
    ppermute x8, starting transfers between devices, across(): return lax.ppermute(value, 'dp', [(k, k ^ m) for k in range(dp_size)])  13.2 us
    pallas_call x2, Pallas kernels, chip_state(): pl.pallas_call(functools.partial(state_kernel, first), name='chip_state',...  11.4 us
    ppermute x3, waiting for transfers between devices, along(): return lax.ppermute(value, 'ctx', [(k, k ^ 2 * m) for k in range(ctx_size)])  10.1 us
    ppermute x3, starting transfers between devices, along(): return lax.ppermute(value, 'ctx', [(k, k ^ 2 * m) for k in range(ctx_size)])  4.45 us
    ppermute x8, waiting for transfers between devices, across(): return lax.ppermute(value, 'dp', [(k, k ^ m) for k in range(dp_size)])  4.08 us
  transfers between devices with their start and end apart: 23, of which 12 were waited for; matrix products, arithmetic and copies ran while one was open for 4% of the time, Pallas kernels for 37%

profile of v1, /device:TPU:0, one launch (start us, length us, event | category | flops | bytes accessed | tf_op | source)
XLA Modules:
  0.0 153.3 jit_solution(8340983225445218885)
XLA Ops:
  0.7 3.8 %slice_select_fusion = (bf16[128,4096]{1,0:T(8,128)(2,1)}, bf16[128,4096]{1,0:T(8,128)(2,1)}) fusion(bf16[128,8192]{1,0:T(8,128)(2,1)} %g_ref.11, bf16[128,8192]{1,0:T(8,128)(2,1)} %x_ref.11, pred[]{:T(512)S(6)} %eq.5), kind=kLoop, calls=%fused_computation.10 | loop fusion | flops 1048576 | bytes 6291457 | tf_op jit(solution)/shard_map/jit(_where)/select_n | solution.py:440
  5.6 2.1 %collective-permute-done.2.far_ref.mf_ref = bf16[128,640]{1,0:T(8,128)(2,1)S(1)} collective-permute-done((bf16[128,640]{1,0:T(8,128)(2,1)S(1)}, bf16[128,640]{1,0:T(8,128)(2,1)S(1)}, u32[]{:S(2)}, u32[]{:S(2)}) %collective-permute-start.2) | collective-permute-done | bytes 163872 | tf_op jit(solution)/shard_map/ppermute | solution.py:421
  8.3 2.0 %prep.1 = (bf16[272,128]{1,0:T(8,128)(2,1)}, bf16[272,128]{1,0:T(8,128)(2,1)}, bf16[128,128]{1,0:T(8,128)(2,1)}, bf16[128,128]{1,0:T(8,128)(2,1)}, f32[128,128]{...) custom-call(s32[1,4]{1,0:T(1,128)} %docs_ref.1, ...), custom_call_target="tpu_custom_call" | custom-call | flops 20000000 | bytes 1000000 | tf_op jit(solution)/shard_map/prep/pallas_call | solution.py:123
  11.4 5.7 %chip_state.3 = (bf16[128,4096]{1,0:T(8,128)(2,1)}, f32[16,4096]{1,0:T(8,128)}) custom-call(bf16[272,128]{1,0:T(8,128)(2,1)} %get-tuple-element.51.whi_ref, bf16[272,128]{1,0:T(8,128)(2,1)} %get-tuple-element.52.wlo_ref, bf16[128,8192]{1,0:T(8,128)(2,1)} %x_ref.11, bf16[128,8192]{1,0:T(8,128)(2,1)} %g_ref.11, bf16[128,4096]{1,0:T(8,128)(2,1)} %copy-done.3, ...), custom_call_target="tpu_custom_call" | custom-call | flops 1073741824 | bytes 4194304 | tf_op jit(solution)/shard_map/chip_state/pallas_call | solution.py:159
  18.5 5.7 %chip_state.2 = (bf16[128,4096]{1,0:T(8,128)(2,1)}, f32[16,4096]{1,0:T(8,128)}) custom-call(bf16[272,128]{1,0:T(8,128)(2,1)} %get-tuple-element.51.whi_ref, bf16[272,128]{1,0:T(8,128)(2,1)} %get-tuple-element.52.wlo_ref, bf16[128,8192]{1,0:T(8,128)(2,1)} %x_ref.11, bf16[128,8192]{1,0:T(8,128)(2,1)} %g_ref.11, bf16[128,4096]{1,0:T(8,128)(2,1)} %copy-done.4, ...), custom_call_target="tpu_custom_call" | custom-call | flops 1073741824 | bytes 4194304 | tf_op jit(solution)/shard_map/chip_state/pallas_call | solution.py:159
  24.1 2.4 %collective-permute-start.9 = (bf16[128,4096]{1,0:T(8,128)(2,1)}, bf16[128,4096]{1,0:T(8,128)(2,1)S(1)}, u32[]{:S(2)}, u32[]{:S(2)}) collective-permute-start(bf16[128,4096]{1,0:T(8,128)(2,1)} %get-tuple-element.69), channel_id=1, source_target_pairs={{1,3},{0,1},{3,5},{2,0},{5,7},{4,2},{7,6},{6,4},{9,11},{8,9},{11,1... | collective-permute-start | bytes 3145736 | tf_op jit(solution)/shard_map/ppermute | solution.py:429
  28.4 4.6 %collective-permute-done.5.refs_0_ = bf16[128,4096]{1,0:T(8,128)(2,1)S(1)} collective-permute-done((bf16[128,4096]{1,0:T(8,128)(2,1)}, bf16[128,4096]{1,0:T(8,128)(2,1)S(1)}, u32[]{:S(2)}, u32[]{:S(2)}) %collective-permute-start.5) | collective-permute-done | bytes 1048608 | tf_op jit(solution)/shard_map/ppermute | solution.py:429
  33.3 10.9 %collective-permute-done.9.refs_0_ = bf16[128,4096]{1,0:T(8,128)(2,1)S(1)} collective-permute-done((bf16[128,4096]{1,0:T(8,128)(2,1)}, bf16[128,4096]{1,0:T(8,128)(2,1)S(1)}, u32[]{:S(2)}, u32[]{:S(2)}) %collective-permute-start.9) | collective-permute-done | bytes 1048608 | tf_op jit(solution)/shard_map/ppermute | solution.py:429
  45.6 9.9 %collective-permute-done.6.refs_1_ = bf16[128,4096]{1,0:T(8,128)(2,1)S(1)} collective-permute-done((bf16[128,4096]{1,0:T(8,128)(2,1)S(1)}, bf16[128,4096]{1,0:T(8,128)(2,1)S(1)}, u32[]{:S(2)}, u32[]{:S(2)}) %collective-permute-start.6) | collective-permute-done | bytes 1048608 | tf_op jit(solution)/shard_map/ppermute | solution.py:429
  56.0 10.8 %collective-permute-done.10.refs_1_ = bf16[128,4096]{1,0:T(8,128)(2,1)} collective-permute-done((bf16[128,4096]{1,0:T(8,128)(2,1)S(1)}, bf16[128,4096]{1,0:T(8,128)(2,1)}, u32[]{:S(2)}, u32[]{:S(2)}) %collective-permute-start.10) | collective-permute-done | bytes 1048608 | tf_op jit(solution)/shard_map/ppermute | solution.py:429
  67.5 3.3 %collective-permute-start = (f32[1]{0:T(128)}, f32[1]{0:T(128)}, u32[]{:S(2)}, u32[]{:S(2)}) collective-permute-start(f32[1]{0:T(128)} %convert_element_type.18), channel_id=1, source_target_pairs={{0,8},{8,0},{16,24},{24,16},{1,9},{9,1},{17,25},{25,17},{2,10},{10... | collective-permute-start | bytes 20 | tf_op jit(solution)/shard_map/ppermute | solution.py:432
  70.8 2.9 %constant_dynamic-slice_fusion.3 = (bf16[128,2048]{1,0:T(8,128)(2,1)}, bf16[128,2048]{1,0:T(8,128)(2,1)}, bf16[128,2048]{1,0:T(8,128)(2,1)}, bf16[128,2048]{1,0:T(8,128)(2,1)}) fusion(bf16[128,8192]{1,0:T(8,128)(2,1)} %param.16, s32[]{:T(128)S(6)} %select_n.90, s32[]{:T(128)S(6)} %select_n.91, s32[]{:T(128)S(6)} %select_n.93, s32[]{:T(128)S(6)} %select_n.92), kind=kLoop, calls=%fused_computation.33 | loop fusion | bytes 4194320 | tf_op jit(solution)/shard_map/dynamic_slice | solution.py:472
  74.3 2.9 %collective-permute-start.1 = (f32[1]{0:T(128)}, f32[1]{0:T(128)}, u32[]{:S(2)}, u32[]{:S(2)}) collective-permute-start(f32[1]{0:T(128)} %add.56), channel_id=1, source_target_pairs={{0,16},{8,24},{16,0},{24,8},{1,17},{9,25},{17,1},{25,9},{2,18},{10... | collective-permute-start | bytes 20 | tf_op jit(solution)/shard_map/ppermute | solution.py:432
  78.7 2.0 %collective-permute-start.14 = (bf16[128,2048]{1,0:T(8,128)(2,1)}, bf16[128,2048]{1,0:T(8,128)(2,1)}, u32[]{:S(2)}, u32[]{:S(2)}) collective-permute-start(bf16[128,2048]{1,0:T(8,128)(2,1)} %get-tuple-element.82), channel_id=1, source_target_pairs={{0,16},{8,24},{16,0},{24,8},{1,17},{9,25},{17,1},{25,9},{2,18},{10... | collective-permute-start | bytes 1572872 | tf_op jit(solution)/shard_map/ppermute | solution.py:432
  82.1 11.3 %within_block.3 = (f32[128,4096]{1,0:T(8,128)}, f32[128,4096]{1,0:T(8,128)}, f32[128,128]{1,0:T(8,128)}, f32[128,128]{1,0:T(8,128)}, f32[128,256]{1,0:T(8,128)}, /*index=5*/f32[128,256]{1,0:T(8,128)}) custom-call(bf16[128,128]{1,0:T(8,128)(2,1)} %get-tuple-element.46.fhi_ref, bf16[128,128]{1,0:T(8,128)(2,1)} %get-tuple-element.47.flo_ref, ...), custom_call_target="tpu_custom_call" | custom-call | flops 1073741824 | bytes 7340032 | tf_op jit(solution)/shard_map/within_block/pallas_call | solution.py:258
  93.5 11.4 %within_block.2 = (f32[128,4096]{1,0:T(8,128)}, f32[128,4096]{1,0:T(8,128)}, f32[128,128]{1,0:T(8,128)}, f32[128,128]{1,0:T(8,128)}, f32[128,256]{1,0:T(8,128)}, /*index=5*/f32[128,256]{1,0:T(8,128)}) custom-call(bf16[128,128]{1,0:T(8,128)(2,1)} %get-tuple-element.46.fhi_ref, bf16[128,128]{1,0:T(8,128)(2,1)} %get-tuple-element.47.flo_ref, ...), custom_call_target="tpu_custom_call" | custom-call | flops 1073741824 | bytes 7340032 | tf_op jit(solution)/shard_map/within_block/pallas_call | solution.py:258
  105.5 10.3 %finish.2 = (bf16[128,8192]{1,0:T(8,128)(2,1)}, bf16[128,512]{1,0:T(8,128)(2,1)}, bf16[128,512]{1,0:T(8,128)(2,1)}, f32[128,128]{1,0:T(8,128)}) custom-call(f32[1,1]{1,0:T(1,128)} %bitcast.weight_ref, bf16[256,128]{1,0:T(8,128)(2,1)} %get-tuple-element.41.khi_ref, bf16[256,128]{1,0:T(8,128)(2,1)} %get-tuple-element.42.klo_ref, ...), custom_call_target="tpu_custom_call" | custom-call | flops 1610612736 | bytes 10485760 | tf_op jit(solution)/shard_map/finish/pallas_call | solution.py:389
  115.8 10.5 %finish.3 = (bf16[128,8192]{1,0:T(8,128)(2,1)}, bf16[128,512]{1,0:T(8,128)(2,1)}, bf16[128,512]{1,0:T(8,128)(2,1)}, f32[128,128]{1,0:T(8,128)}) custom-call(f32[1,1]{1,0:T(1,128)} %bitcast.weight_ref, bf16[256,128]{1,0:T(8,128)(2,1)} %get-tuple-element.41.khi_ref, ...), custom_call_target="tpu_custom_call", output_to_operand_aliasing={{0}: (22, {}), {1}: (23, {}), {2}: (24, {})} | custom-call | flops 1610612736 | bytes 10485760 | tf_op jit(solution)/shard_map/finish/pallas_call | solution.py:389
  127.2 1.9 %collective-permute-start.17 = (bf16[128,128]{1,0:T(8,128)(2,1)S(1)}, bf16[128,128]{1,0:T(8,128)(2,1)S(1)}, u32[]{:S(2)}, u32[]{:S(2)}) collective-permute-start(bf16[128,128]{1,0:T(8,128)(2,1)S(1)} %convert_element_type.23), channel_id=1, source_target_pairs={{0,16},{8,24},{16,0},{24,8},{1,17},{9,25},{17,1},{25,9},{2,18},{10... | collective-permute-start | bytes 98312 | tf_op jit(solution)/shard_map/ppermute | solution.py:432
  131.2 2.8 %collective-permute-done.18 = bf16[128,128]{1,0:T(8,128)(2,1)S(1)} collective-permute-done((bf16[128,128]{1,0:T(8,128)(2,1)S(1)}, bf16[128,128]{1,0:T(8,128)(2,1)S(1)}, u32[]{:S(2)}, u32[]{:S(2)}) %collective-permute-start.18) | collective-permute-done | bytes 32800 | tf_op jit(solution)/shard_map/ppermute | solution.py:432
  134.0 1.9 %fusion = f32[2048,128]{1,0:T(8,128)S(1)} fusion(bf16[128,2048]{1,0:T(8,128)(2,1)S(1)} %collective-permute-done.15, bf16[128,2048]{1,0:T(8,128)(2,1)} %collective-permute-done.14, bf16[128,2048]{1,0:T(8,128)(2,1)} %collective-permute-done.13, bf16[128,2048]{1,0:T(8,128)(2,1)S(1)} %copy-done.8, bf16[128,128]{1,0:T(8,128)(2,1)S(1)} %collective-permute-done.18, ...), kind=kOutput, calls=%fused_computation | convolution fusion | flops 277348352 | bytes 3276800 | tf_op jit(solution)/shard_map/dot_general | solution.py:493
  136.1 1.9 %collective-permute-done.19 = f32[4,256,128]{2,1,0:T(8,128)S(1)} collective-permute-done((f32[4,256,128]{2,1,0:T(8,128)S(1)}, f32[4,256,128]{2,1,0:T(8,128)S(1)}, u32[]{:S(2)}, u32[]{:S(2)}) %collective-permute-start.19) | collective-permute-done | bytes 524320 | tf_op jit(solution)/shard_map/ppermute | solution.py:421
  142.5 3.1 %collective-permute-done.20 = f32[256,128]{1,0:T(8,128)S(1)} collective-permute-done((f32[256,128]{1,0:T(8,128)S(1)}, f32[256,128]{1,0:T(8,128)S(1)}, u32[]{:S(2)}, u32[]{:S(2)}) %collective-permute-start.20) | collective-permute-done | bytes 131104 | tf_op jit(solution)/shard_map/ppermute | solution.py:435
  145.6 7.0 %collective-permute-done.21 = f32[256,128]{1,0:T(8,128)S(1)} collective-permute-done((f32[256,128]{1,0:T(8,128)S(1)}, f32[256,128]{1,0:T(8,128)S(1)}, u32[]{:S(2)}, u32[]{:S(2)}) %collective-permute-start.21) | collective-permute-done | bytes 131104 | tf_op jit(solution)/shard_map/ppermute | solution.py:435
  (66 shorter events, 19.2 us)
Async XLA Ops:
  4.4 5.9 %collective-permute-start.4 = (bf16[128,4096]{1,0:T(8,128)(2,1)}, bf16[128,4096]{1,0:T(8,128)(2,1)S(1)}, u32[]{:S(2)}, u32[]{:S(2)}) collective-permute-start(bf16[128,4096]{1,0:T(8,128)(2,1)} %get-tuple-element.77), channel_id=1, source_target_pairs={{0,1},{1,0},{2,3},{3,2},{4,5},{5,4},{6,7},{7,6},{8,9},{9,8},{10,11... | collective-permute-start | bytes 3145736 | tf_op jit(solution)/shard_map/ppermute | solution.py:421
  5.0 2.7 %collective-permute-start.2 = (bf16[128,640]{1,0:T(8,128)(2,1)S(1)}, bf16[128,640]{1,0:T(8,128)(2,1)S(1)}, u32[]{:S(2)}, u32[]{:S(2)}) collective-permute-start(bf16[128,640]{1,0:T(8,128)(2,1)S(1)} %pad_maximum_fusion), channel_id=1, source_target_pairs={{0,1},{1,0},{2,3},{3,2},{4,5},{5,4},{6,7},{7,6},{8,9},{9,8},{10,11... | collective-permute-start | bytes 491528 | tf_op jit(solution)/shard_map/ppermute | solution.py:421
  5.1 12.4 %collective-permute-start.3 = (bf16[128,4096]{1,0:T(8,128)(2,1)}, bf16[128,4096]{1,0:T(8,128)(2,1)S(1)}, u32[]{:S(2)}, u32[]{:S(2)}) collective-permute-start(bf16[128,4096]{1,0:T(8,128)(2,1)} %get-tuple-element.78), channel_id=1, source_target_pairs={{0,1},{1,0},{2,3},{3,2},{4,5},{5,4},{6,7},{7,6},{8,9},{9,8},{10,11... | collective-permute-start | bytes 3145736 | tf_op jit(solution)/shard_map/ppermute | solution.py:421
  17.1 15.9 %collective-permute-start.5 = (bf16[128,4096]{1,0:T(8,128)(2,1)}, bf16[128,4096]{1,0:T(8,128)(2,1)S(1)}, u32[]{:S(2)}, u32[]{:S(2)}) collective-permute-start(bf16[128,4096]{1,0:T(8,128)(2,1)} %get-tuple-element.63), channel_id=1, source_target_pairs={{1,3},{0,1},{3,5},{2,0},{5,7},{4,2},{7,6},{6,4},{9,11},{8,9},{11,1... | collective-permute-start | bytes 3145736 | tf_op jit(solution)/shard_map/ppermute | solution.py:429
  24.1 20.1 %collective-permute-start.9 = (bf16[128,4096]{1,0:T(8,128)(2,1)}, bf16[128,4096]{1,0:T(8,128)(2,1)S(1)}, u32[]{:S(2)}, u32[]{:S(2)}) collective-permute-start(bf16[128,4096]{1,0:T(8,128)(2,1)} %get-tuple-element.69), channel_id=1, source_target_pairs={{1,3},{0,1},{3,5},{2,0},{5,7},{4,2},{7,6},{6,4},{9,11},{8,9},{11,1... | collective-permute-start | bytes 3145736 | tf_op jit(solution)/shard_map/ppermute | solution.py:429
  33.3 22.2 %collective-permute-start.6 = (bf16[128,4096]{1,0:T(8,128)(2,1)S(1)}, bf16[128,4096]{1,0:T(8,128)(2,1)S(1)}, u32[]{:S(2)}, u32[]{:S(2)}) collective-permute-start(bf16[128,4096]{1,0:T(8,128)(2,1)S(1)} %select_convert_fusion.1), channel_id=1, source_target_pairs={{1,3},{0,1},{3,5},{2,0},{5,7},{4,2},{7,6},{6,4},{9,11},{8,9},{11,1... | collective-permute-start | bytes 3145736 | tf_op jit(solution)/shard_map/ppermute | solution.py:429
  44.3 29.4 %copy-start.5 = (bf16[128,4096]{1,0:T(8,128)(2,1)}, bf16[128,4096]{1,0:T(8,128)(2,1)S(1)}, u32[]{:S(2)}) copy-start(bf16[128,4096]{1,0:T(8,128)(2,1)S(1)} %collective-permute-done.9.refs_0_) | copy-start | bytes 3145732
  44.5 22.3 %collective-permute-start.10 = (bf16[128,4096]{1,0:T(8,128)(2,1)S(1)}, bf16[128,4096]{1,0:T(8,128)(2,1)}, u32[]{:S(2)}, u32[]{:S(2)}) collective-permute-start(bf16[128,4096]{1,0:T(8,128)(2,1)S(1)} %select_convert_fusion), channel_id=1, source_target_pairs={{1,3},{0,1},{3,5},{2,0},{5,7},{4,2},{7,6},{6,4},{9,11},{8,9},{11,1... | collective-permute-start | bytes 3145736 | tf_op jit(solution)/shard_map/ppermute | solution.py:429
  44.6 34.1 %collective-permute-start.7 = (bf16[128,4096]{1,0:T(8,128)(2,1)S(1)}, bf16[128,4096]{1,0:T(8,128)(2,1)}, u32[]{:S(2)}, u32[]{:S(2)}) collective-permute-start(bf16[128,4096]{1,0:T(8,128)(2,1)S(1)} %collective-permute-done.5.refs_0_), channel_id=1, source_target_pairs={{0,1},{1,0},{2,3},{3,2},{4,5},{5,4},{6,7},{7,6},{8,9},{9,8},{10,11... | collective-permute-start | bytes 3145736 | tf_op jit(solution)/shard_map/ppermute | solution.py:421
  55.5 25.2 %collective-permute-start.8 = (bf16[128,4096]{1,0:T(8,128)(2,1)S(1)}, bf16[128,4096]{1,0:T(8,128)(2,1)}, u32[]{:S(2)}, u32[]{:S(2)}) collective-permute-start(bf16[128,4096]{1,0:T(8,128)(2,1)S(1)} %collective-permute-done.6.refs_1_), channel_id=1, source_target_pairs={{0,1},{1,0},{2,3},{3,2},{4,5},{5,4},{6,7},{7,6},{8,9},{9,8},{10,11... | collective-permute-start | bytes 3145736 | tf_op jit(solution)/shard_map/ppermute | solution.py:421
  55.5 60.3 %collective-permute-start.11 = (bf16[128,4096]{1,0:T(8,128)(2,1)S(1)}, bf16[128,4096]{1,0:T(8,128)(2,1)}, u32[]{:S(2)}, u32[]{:S(2)}) collective-permute-start(bf16[128,4096]{1,0:T(8,128)(2,1)S(1)} %collective-permute-done.9.refs_0_), channel_id=1, source_target_pairs={{0,1},{1,0},{2,3},{3,2},{4,5},{5,4},{6,7},{7,6},{8,9},{9,8},{10,11... | collective-permute-start | bytes 3145736 | tf_op jit(solution)/shard_map/ppermute | solution.py:421
  66.8 48.9 %collective-permute-start.12 = (bf16[128,4096]{1,0:T(8,128)(2,1)}, bf16[128,4096]{1,0:T(8,128)(2,1)}, u32[]{:S(2)}, u32[]{:S(2)}) collective-permute-start(bf16[128,4096]{1,0:T(8,128)(2,1)} %collective-permute-done.10.refs_1_), channel_id=1, source_target_pairs={{0,1},{1,0},{2,3},{3,2},{4,5},{5,4},{6,7},{7,6},{8,9},{9,8},{10,11... | collective-permute-start | bytes 3145736 | tf_op jit(solution)/shard_map/ppermute | solution.py:421
  67.5 6.2 %collective-permute-start = (f32[1]{0:T(128)}, f32[1]{0:T(128)}, u32[]{:S(2)}, u32[]{:S(2)}) collective-permute-start(f32[1]{0:T(128)} %convert_element_type.18), channel_id=1, source_target_pairs={{0,8},{8,0},{16,24},{24,16},{1,9},{9,1},{17,25},{25,17},{2,10},{10... | collective-permute-start | bytes 20 | tf_op jit(solution)/shard_map/ppermute | solution.py:432
  74.3 3.6 %collective-permute-start.1 = (f32[1]{0:T(128)}, f32[1]{0:T(128)}, u32[]{:S(2)}, u32[]{:S(2)}) collective-permute-start(f32[1]{0:T(128)} %add.56), channel_id=1, source_target_pairs={{0,16},{8,24},{16,0},{24,8},{1,17},{9,25},{17,1},{25,9},{2,18},{10... | collective-permute-start | bytes 20 | tf_op jit(solution)/shard_map/ppermute | solution.py:432
  77.9 51.3 %collective-permute-start.13 = (bf16[128,2048]{1,0:T(8,128)(2,1)}, bf16[128,2048]{1,0:T(8,128)(2,1)}, u32[]{:S(2)}, u32[]{:S(2)}) collective-permute-start(bf16[128,2048]{1,0:T(8,128)(2,1)} %get-tuple-element.80), channel_id=1, source_target_pairs={{0,8},{8,0},{16,24},{24,16},{1,9},{9,1},{17,25},{25,17},{2,10},{10... | collective-permute-start | bytes 1572872 | tf_op jit(solution)/shard_map/ppermute | solution.py:432
  78.7 51.9 %collective-permute-start.14 = (bf16[128,2048]{1,0:T(8,128)(2,1)}, bf16[128,2048]{1,0:T(8,128)(2,1)}, u32[]{:S(2)}, u32[]{:S(2)}) collective-permute-start(bf16[128,2048]{1,0:T(8,128)(2,1)} %get-tuple-element.82), channel_id=1, source_target_pairs={{0,16},{8,24},{16,0},{24,8},{1,17},{9,25},{17,1},{25,9},{2,18},{10... | collective-permute-start | bytes 1572872 | tf_op jit(solution)/shard_map/ppermute | solution.py:432
  80.7 49.9 %collective-permute-start.15 = (bf16[128,2048]{1,0:T(8,128)(2,1)}, bf16[128,2048]{1,0:T(8,128)(2,1)S(1)}, u32[]{:S(2)}, u32[]{:S(2)}) collective-permute-start(bf16[128,2048]{1,0:T(8,128)(2,1)} %get-tuple-element.81), channel_id=1, source_target_pairs={{0,24},{8,16},{16,8},{24,0},{1,25},{9,17},{17,9},{25,1},{2,26},{10... | collective-permute-start | bytes 1572872 | tf_op jit(solution)/shard_map/ppermute | solution.py:432
  127.1 3.9 %collective-permute-start.16 = (bf16[128,128]{1,0:T(8,128)(2,1)S(1)}, bf16[128,128]{1,0:T(8,128)(2,1)S(1)}, u32[]{:S(2)}, u32[]{:S(2)}) collective-permute-start(bf16[128,128]{1,0:T(8,128)(2,1)S(1)} %convert_element_type.23), channel_id=1, source_target_pairs={{0,8},{8,0},{16,24},{24,16},{1,9},{9,1},{17,25},{25,17},{2,10},{10... | collective-permute-start | bytes 98312 | tf_op jit(solution)/shard_map/ppermute | solution.py:432
  127.2 3.9 %collective-permute-start.17 = (bf16[128,128]{1,0:T(8,128)(2,1)S(1)}, bf16[128,128]{1,0:T(8,128)(2,1)S(1)}, u32[]{:S(2)}, u32[]{:S(2)}) collective-permute-start(bf16[128,128]{1,0:T(8,128)(2,1)S(1)} %convert_element_type.23), channel_id=1, source_target_pairs={{0,16},{8,24},{16,0},{24,8},{1,17},{9,25},{17,1},{25,9},{2,18},{10... | collective-permute-start | bytes 98312 | tf_op jit(solution)/shard_map/ppermute | solution.py:432
  129.2 4.8 %collective-permute-start.18 = (bf16[128,128]{1,0:T(8,128)(2,1)S(1)}, bf16[128,128]{1,0:T(8,128)(2,1)S(1)}, u32[]{:S(2)}, u32[]{:S(2)}) collective-permute-start(bf16[128,128]{1,0:T(8,128)(2,1)S(1)} %convert_element_type.23), channel_id=1, source_target_pairs={{0,24},{8,16},{16,8},{24,0},{1,25},{9,17},{17,9},{25,1},{2,26},{10... | collective-permute-start | bytes 98312 | tf_op jit(solution)/shard_map/ppermute | solution.py:432
  136.0 2.0 %collective-permute-start.19 = (f32[4,256,128]{2,1,0:T(8,128)S(1)}, f32[4,256,128]{2,1,0:T(8,128)S(1)}, u32[]{:S(2)}, u32[]{:S(2)}) collective-permute-start(f32[4,256,128]{2,1,0:T(8,128)S(1)} %dynamic-slice_bitcast_fusion), channel_id=1, source_target_pairs={{0,1},{1,0},{2,3},{3,2},{4,5},{5,4},{6,7},{7,6},{8,9},{9,8},{10,11... | collective-permute-start | bytes 1572872 | tf_op jit(solution)/shard_map/ppermute | solution.py:421
  138.1 7.5 %collective-permute-start.20 = (f32[256,128]{1,0:T(8,128)S(1)}, f32[256,128]{1,0:T(8,128)S(1)}, u32[]{:S(2)}, u32[]{:S(2)}) collective-permute-start(f32[256,128]{1,0:T(8,128)S(1)} %get-tuple-element.83), channel_id=1, source_target_pairs={{0,2},{1,3},{2,0},{3,1},{4,6},{5,7},{6,4},{7,5},{8,10},{9,11},{10,... | collective-permute-start | bytes 393224 | tf_op jit(solution)/shard_map/ppermute | solution.py:435
  139.7 12.9 %collective-permute-start.21 = (f32[256,128]{1,0:T(8,128)S(1)}, f32[256,128]{1,0:T(8,128)S(1)}, u32[]{:S(2)}, u32[]{:S(2)}) collective-permute-start(f32[256,128]{1,0:T(8,128)S(1)} %get-tuple-element.85), channel_id=1, source_target_pairs={{0,4},{1,5},{2,6},{3,7},{4,0},{5,1},{6,2},{7,3},{8,12},{9,13},{10,... | collective-permute-start | bytes 393224 | tf_op jit(solution)/shard_map/ppermute | solution.py:435
  141.3 11.3 %collective-permute-start.22 = (f32[256,128]{1,0:T(8,128)S(1)}, f32[256,128]{1,0:T(8,128)S(1)}, u32[]{:S(2)}, u32[]{:S(2)}) collective-permute-start(f32[256,128]{1,0:T(8,128)S(1)} %get-tuple-element.84), channel_id=1, source_target_pairs={{0,6},{1,7},{2,4},{3,5},{4,2},{5,3},{6,0},{7,1},{8,14},{9,15},{10,... | collective-permute-start | bytes 393224 | tf_op jit(solution)/shard_map/ppermute | solution.py:435
  (10 other events, 72.3 us)
